TPU v7x, 32 devices: a whole 2x2x4 slice. The times are simulated.
32 devices in a mesh: row: 2 (over x), col: 16 (over z, y, core).
Axes of the slice: x: 2, y: 2, z: 4, core: 2. Of those that a mesh axis runs over, the one named last changes fastest.
Arguments:
- coords: float32 [64, 3, 256], P(('row', 'col')), may hold values from 0 to 8, as said below
- noise_var: float32 [64, 256], P(('row', 'col')), may hold values from 0.1 to 1
- right_side: float32 [64, 8, 256], P(('row', 'col')), may hold values from -32 to 32
- start_guess: float32 [64, 8, 256], P(('row', 'col')), may hold values from -3 to 3
- tile_pairs: int32 [2, 16, 2, 63], P('row', 'col'), may hold values from -1 to 31, as said below
Outputs:
- solution_field: float32 [64, 8, 256], P(('row', 'col'))
- residual: float32 [64, 8, 256], P(('row', 'col'))
Inputs may be any that keep to these rules, and one draw needn't show every extreme that they name: `coords`: each tile's points lie within one unit cell of the integer lattice, and distinct tiles lie in distinct cells. `tile_pairs`: each device's list holds every pair of its block whose cells differ by at most one in each coordinate, each pair once and no other; listed entries come first, then entries of -1 in both rows.
All inputs are finite; a program needn't handle non-finite values.
Results may differ from a plain program's by a relative error of at most 0.0003.
Values sent between devices are 32-bit elements; how exact they have to be, the bound alone decides.
A program may use at most 64 MiB of HBM per device.

v0:
```python
import jax
import jax.numpy as jnp
from jax import lax
from jax.sharding import PartitionSpec as P

ITERS = 3
pair_group = 2


def wendland(left_points, right_points):
    squared = jnp.zeros(
        (left_points.shape[0], left_points.shape[2], right_points.shape[2]), jnp.float32
    )
    for component in range(3):
        spacing = left_points[:, component, :, None] - right_points[:, component, None, :]
        squared = squared + spacing * spacing
    distance = jnp.sqrt(squared)
    remain = jnp.maximum(1.0 - distance, 0.0)
    return remain**4 * (4.0 * distance + 1.0)


def squares(residual):
    return lax.psum(jnp.sum(residual * residual, axis=(0, 2)), ("row", "col"))


def shards(coords, noise_var, right_side, start_guess, tile_pairs):
    row_points = lax.all_gather(coords, "col", axis=0, tiled=True)
    col_points = lax.all_gather(coords, "row", axis=0, tiled=True)
    row_count = row_points.shape[0]
    listed = tile_pairs[0, 0]
    usable = listed[0] >= 0
    sort_key = jnp.where(usable, listed[0], row_count)
    sorted_index = jnp.argsort(sort_key, stable=True)
    sorted_rows = jnp.concatenate(
        [sort_key[sorted_index], jnp.full((pair_group,), row_count, jnp.int32)]
    )
    sorted_cols = jnp.concatenate(
        [jnp.where(usable, listed[1], 0)[sorted_index], jnp.zeros((pair_group,), jnp.int32)]
    )

    def pair_range(first_row, row_number):
        first = jnp.sum(sorted_rows < first_row)
        last = jnp.sum(sorted_rows < first_row + row_number)
        return (first, last, (last - first + pair_group - 1) // pair_group)

    def group_weights(position, last):
        indices = position + jnp.arange(pair_group, dtype=jnp.int32)
        rows_group = lax.dynamic_slice_in_dim(sorted_rows, position, pair_group)
        cols_group = lax.dynamic_slice_in_dim(sorted_cols, position, pair_group)
        inside = (indices < last).astype(jnp.float32)
        safe_rows = jnp.minimum(rows_group, row_count - 1)
        weights = wendland(row_points[safe_rows], col_points[cols_group]) * inside[:, None, None]
        return (weights, safe_rows, cols_group)

    def apply_operator(vectors):
        empty = jnp.zeros((col_points.shape[0],) + vectors.shape[1:], jnp.float32)
        pieces = lax.all_gather(vectors, "col", axis=0, tiled=True)
        number = pieces.shape[0]
        first, last, turns = pair_range(jnp.int32(0), number)

        def visit(turn, running):
            weights, safe_rows, cols_group = group_weights(first + pair_group * turn, last)
            local_rows = jnp.clip(safe_rows, 0, number - 1)
            product = jnp.einsum(
                "pab,psa->psb", weights, pieces[local_rows], precision=lax.Precision.HIGHEST
            )
            return running.at[cols_group].add(product)

        gathered_sum = lax.fori_loop(0, turns, visit, empty)
        coupled = lax.psum_scatter(gathered_sum, "row", scatter_dimension=0, tiled=True)
        return coupled + noise_var[:, None, :] * vectors

    solution_field = start_guess
    residual = right_side - apply_operator(start_guess)
    direction = residual
    norm_now = squares(residual)
    for iteration in range(ITERS):
        applied = apply_operator(direction)
        step_size = norm_now / lax.psum(jnp.sum(direction * applied, axis=(0, 2)), ("row", "col"))
        solution_field = solution_field + step_size[None, :, None] * direction
        residual = residual - step_size[None, :, None] * applied
        norm_next = squares(residual)
        direction = residual + (norm_next / norm_now)[None, :, None] * direction
        norm_now = norm_next
    return (solution_field, residual)


def solution(mesh):
    placed = (
        P(("row", "col"), None, None),
        P(("row", "col"), None),
        P(("row", "col"), None, None),
        P(("row", "col"), None, None),
        P("row", "col", None, None),
    )
    return jax.shard_map(
        shards,
        mesh=mesh,
        in_specs=placed,
        out_specs=(P(("row", "col"), None, None), P(("row", "col"), None, None)),
        check_vma=False,
    )
```

profile of v0, /device:TPU:0, one launch (start us, length us, event | category | flops | bytes accessed | tf_op | source)
XLA Modules:
  0.0 646.0 jit_solution(4284149621219089081)
XLA Ops:
  8.0 2.0 sort.17
  13.5 23.5 %all_gather.19 = f32[32,3,256]{2,1,0:T(4,128)S(1)} all-gather(f32[2,3,256]{2,1,0:T(4,128)S(1)} %copy.11), channel_id=1, replica_groups=mesh['row'=2,'col'=16] {'col'}, dimensions={0}, use_global_device_ids=true | all-gather | bytes 104448 | tf_op jit(solution)/shard_map/all_gather | solution.py:27
  36.9 4.3 all_gather.20
  42.1 17.8 %all_gather.18 = f32[32,8,256]{2,1,0:T(8,128)S(1)} all-gather(f32[2,8,256]{2,1,0:T(8,128)S(1)} %copy-done.5), channel_id=1, replica_groups=mesh['row'=2,'col'=16] {'col'}, dimensions={0}, use_global_device_ids=true | all-gather | bytes 278528 | tf_op jit(solution)/shard_map/all_gather | solution.py:57
  59.9 55.7 %while.40 = (s32[]{:T(128)}, f32[4,8,256]{2,1,0:T(8,128)S(1)}, s32[]{:T(128)}, s32[]{:T(128)}, s32[65]{0:T(128)S(1)}, /*index=5*/s32[65]{0:T(128)S(1)}, f32[32,8...) while((s32[]{:T(128)}, f32[4,8,256]{2,1,0:T(8,128)S(1)}, ...), condition=%wide.region_5.6_spmd, body=%wide.region_3.5_spmd.sunk | while | flops 14687269 | bytes 213307 | solution.py:69
  63.1 0.8 fusion.162
  67.8 0.8 fusion.162
  77.1 0.8 fusion.162
  81.7 0.8 fusion.162
  86.3 0.8 fusion.162
  116.3 22.8 %reduce-scatter.5.cloned.1.call-done = f32[2,8,256]{2,1,0:T(8,128)} async-done(((f32[4,8,256]{2,1,0:T(8,128)}), f32[2,8,256]{2,1,0:T(8,128)}) %reduce-scatter.5.cloned.1.call-update) | async-done | bytes 16400 | tf_op jit(solution)/shard_map/reduce_scatter | solution.py:70
  139.9 22.0 %all_gather.21 = f32[32,8,256]{2,1,0:T(8,128)S(1)} all-gather(f32[2,8,256]{2,1,0:T(8,128)S(1)} %add_subtract_fusion), channel_id=1, replica_groups=mesh['row'=2,'col'=16] {'col'}, dimensions={0}, use_global_device_ids=true | all-gather | bytes 278528 | tf_op jit(solution)/shard_map/all_gather | solution.py:57
  161.9 55.7 %while.41 = (s32[]{:T(128)}, f32[4,8,256]{2,1,0:T(8,128)S(1)}, s32[]{:T(128)}, s32[]{:T(128)}, s32[65]{0:T(128)S(1)}, /*index=5*/s32[65]{0:T(128)S(1)}, f32[32,8...) while((s32[]{:T(128)}, f32[4,8,256]{2,1,0:T(8,128)S(1)}, ...), condition=%wide.region_11.12_spmd, body=%wide.region_9.11_spmd.sunk | while | flops 14687269 | bytes 213307 | solution.py:69
  165.1 0.8 fusion.167
  169.7 0.8 fusion.167
  174.4 0.8 fusion.167
  179.0 0.8 fusion.167
  183.7 0.8 fusion.167
  188.3 0.8 fusion.167
  193.0 0.8 fusion.167
  197.6 0.8 fusion.167
  202.2 0.8 fusion.167
  206.9 0.8 fusion.167
  211.5 0.8 fusion.167
  216.2 0.8 fusion.167
  218.3 20.3 %reduce-scatter.7.cloned.1.call-done = f32[2,8,256]{2,1,0:T(8,128)} async-done(((f32[4,8,256]{2,1,0:T(8,128)}), f32[2,8,256]{2,1,0:T(8,128)}) %reduce-scatter.7.cloned.1.call-update) | async-done | bytes 16400 | tf_op jit(solution)/shard_map/reduce_scatter | solution.py:70
  238.6 0.9 multiply_reduce_fusion.4
  239.5 39.3 %all-reduce.2 = (f32[8]{0:T(128)S(1)}, f32[8]{0:T(128)S(1)}) all-reduce(f32[8]{0:T(128)S(1)} %get-tuple-element.221, f32[8]{0:T(128)S(1)} %get-tuple-element.220), channel_id=1, replica_groups=mesh['row'=2,'col'=16] {'row','col'}, use_global_device_ids=true, to_apply=%region_8.9 | all-reduce | flops 16 | bytes 128 | tf_op jit(solution)/shard_map/psum | solution.py:23
  279.1 40.9 %psum.44 = f32[8]{0:T(128)S(1)} all-reduce(f32[8]{0:T(128)S(1)} %multiply_reduce_fusion.3), channel_id=1, replica_groups=mesh['row'=2,'col'=16] {'row','col'}, use_global_device_ids=true, to_apply=%region_16.17 | all-reduce | flops 8 | bytes 64 | tf_op jit(solution)/shard_map/psum | solution.py:23
  320.1 21.8 %all_gather.22 = f32[32,8,256]{2,1,0:T(8,128)S(1)} all-gather(f32[2,8,256]{2,1,0:T(8,128)S(1)} %multiply_add_fusion.4), channel_id=1, replica_groups=mesh['row'=2,'col'=16] {'col'}, dimensions={0}, use_global_device_ids=true | all-gather | bytes 278528 | tf_op jit(solution)/shard_map/all_gather | solution.py:57
  341.9 55.7 %while.42 = (s32[]{:T(128)}, f32[4,8,256]{2,1,0:T(8,128)S(1)}, s32[]{:T(128)}, s32[]{:T(128)}, s32[65]{0:T(128)S(1)}, /*index=5*/s32[65]{0:T(128)S(1)}, f32[32,8...) while((s32[]{:T(128)}, f32[4,8,256]{2,1,0:T(8,128)S(1)}, ...), condition=%wide.region_19.20_spmd, body=%wide.region_17.19_spmd.sunk | while | flops 14687269 | bytes 213307 | solution.py:69
  345.1 0.8 fusion.172
  349.8 0.8 fusion.172
  354.4 0.8 fusion.172
  359.0 0.8 fusion.172
  363.7 0.8 fusion.172
  368.3 0.8 fusion.172
  373.0 0.8 fusion.172
  377.6 0.8 fusion.172
  382.3 0.8 fusion.172
  386.9 0.8 fusion.172
  391.6 0.8 fusion.172
  396.2 0.8 fusion.172
  398.3 20.3 %reduce-scatter.9.cloned.1.call-done = f32[2,8,256]{2,1,0:T(8,128)} async-done(((f32[4,8,256]{2,1,0:T(8,128)}), f32[2,8,256]{2,1,0:T(8,128)}) %reduce-scatter.9.cloned.1.call-update) | async-done | bytes 16400 | tf_op jit(solution)/shard_map/reduce_scatter | solution.py:70
  418.6 0.9 multiply_reduce_fusion.2
  419.5 39.3 %psum.45 = f32[8]{0:T(128)S(1)} all-reduce(f32[8]{0:T(128)S(1)} %multiply_reduce_fusion.2), channel_id=1, replica_groups=mesh['row'=2,'col'=16] {'row','col'}, use_global_device_ids=true, to_apply=%region_22.23 | all-reduce | flops 8 | bytes 64 | tf_op jit(solution)/shard_map/psum | solution.py:79
  459.0 41.0 %psum.46 = f32[8]{0:T(128)S(1)} all-reduce(f32[8]{0:T(128)S(1)} %get-tuple-element.306), channel_id=1, replica_groups=mesh['row'=2,'col'=16] {'row','col'}, use_global_device_ids=true, to_apply=%region_24.25 | all-reduce | flops 8 | bytes 64 | tf_op jit(solution)/shard_map/psum | solution.py:23
  500.1 21.8 %all_gather.23 = f32[32,8,256]{2,1,0:T(8,128)S(1)} all-gather(f32[2,8,256]{2,1,0:T(8,128)S(1)} %multiply_add_fusion.2), channel_id=1, replica_groups=mesh['row'=2,'col'=16] {'col'}, dimensions={0}, use_global_device_ids=true | all-gather | bytes 278528 | tf_op jit(solution)/shard_map/all_gather | solution.py:57
  521.9 55.7 %while.43 = (s32[]{:T(128)}, f32[4,8,256]{2,1,0:T(8,128)S(1)}, s32[]{:T(128)}, s32[]{:T(128)}, s32[65]{0:T(128)S(1)}, /*index=5*/s32[65]{0:T(128)S(1)}, f32[32,8...) while((s32[]{:T(128)}, f32[4,8,256]{2,1,0:T(8,128)S(1)}, ...), condition=%wide.region_27.28_spmd, body=%wide.region_25.27_spmd.sunk | while | flops 14687269 | bytes 213307 | solution.py:69
  525.1 0.8 fusion.177
  529.7 0.8 fusion.177
  534.4 0.8 fusion.177
  539.0 0.8 fusion.177
  543.7 0.8 fusion.177
  548.3 0.8 fusion.177
  553.0 0.8 fusion.177
  557.6 0.8 fusion.177
  562.2 0.8 fusion.177
  566.9 0.8 fusion.177
  571.5 0.8 fusion.177
  576.2 0.8 fusion.177
  578.3 20.3 %reduce-scatter.11.cloned.1.call-done = f32[2,8,256]{2,1,0:T(8,128)} async-done(((f32[4,8,256]{2,1,0:T(8,128)}), f32[2,8,256]{2,1,0:T(8,128)}) %reduce-scatter.11.cloned.1.call-update) | async-done | bytes 16400 | tf_op jit(solution)/shard_map/reduce_scatter | solution.py:70
  598.6 0.9 multiply_reduce_fusion
  599.5 39.3 %psum.47 = f32[8]{0:T(128)S(1)} all-reduce(f32[8]{0:T(128)S(1)} %multiply_reduce_fusion), channel_id=1, replica_groups=mesh['row'=2,'col'=16] {'row','col'}, use_global_device_ids=true, to_apply=%region_30.31 | all-reduce | flops 8 | bytes 64 | tf_op jit(solution)/shard_map/psum | solution.py:79
  (877 shorter events, 161.6 us)
Async XLA Ops:
  7.2 132.0 %reduce-scatter.5.cloned.1.call-start = ((), (), s32[]{:S(2)}) async-start(), calls=%async_computation.4 | async-start | bytes 49152 | tf_op jit(solution)/shard_map/reduce_scatter | solution.py:70
  12.8 0.7 copy-start.10
  41.3 0.8 copy-start.5
  115.7 0.6 copy-start.1
  115.7 23.5 %copy-start.6 = (f32[2,256]{1,0:T(2,128)S(1)}, f32[2,256]{1,0:T(2,128)}, u32[]{:S(2)}) copy-start(f32[2,256]{1,0:T(2,128)} %param.14) | copy-start | bytes 6148
  115.7 23.5 %copy-start.9 = (f32[2,8,256]{2,1,0:T(8,128)S(1)}, f32[2,8,256]{2,1,0:T(8,128)}, u32[]{:S(2)}) copy-start(f32[2,8,256]{2,1,0:T(8,128)} %param.15) | copy-start | bytes 49156
  116.3 122.3 %reduce-scatter.7.cloned.1.call-start = ((), (), s32[]{:S(2)}) async-start(), calls=%async_computation.5 | async-start | bytes 49152 | tf_op jit(solution)/shard_map/reduce_scatter | solution.py:70
  217.6 0.6 copy-start.2
  218.2 200.4 %reduce-scatter.9.cloned.1.call-start = ((), (), s32[]{:S(2)}) async-start(), calls=%async_computation.6 | async-start | bytes 49152 | tf_op jit(solution)/shard_map/reduce_scatter | solution.py:70
  238.6 40.3 %copy-start.4 = (f32[2,8,256]{2,1,0:T(8,128)S(1)}, f32[2,8,256]{2,1,0:T(8,128)}, u32[]{:S(2)}) copy-start(f32[2,8,256]{2,1,0:T(8,128)} %reduce-scatter.7.cloned.1.call-done) | copy-start | bytes 49156
  397.6 0.6 copy-start.3
  398.3 200.3 %reduce-scatter.11.cloned.1.call-start = ((), (), s32[]{:S(2)}) async-start(), calls=%async_computation.7 | async-start | bytes 49152 | tf_op jit(solution)/shard_map/reduce_scatter | solution.py:70
  418.6 40.2 %copy-start.8 = (f32[2,8,256]{2,1,0:T(8,128)S(1)}, f32[2,8,256]{2,1,0:T(8,128)}, u32[]{:S(2)}) copy-start(f32[2,8,256]{2,1,0:T(8,128)} %reduce-scatter.9.cloned.1.call-done) | copy-start | bytes 49156
  577.6 0.6 copy-start
  598.6 40.2 %copy-start.7 = (f32[2,8,256]{2,1,0:T(8,128)S(1)}, f32[2,8,256]{2,1,0:T(8,128)}, u32[]{:S(2)}) copy-start(f32[2,8,256]{2,1,0:T(8,128)} %reduce-scatter.11.cloned.1.call-done) | copy-start | bytes 49156
Sparse Core Ops, SparseCore 0:
  116.4 22.6 reduce-scatter.4
  218.4 20.1 reduce-scatter.6
  398.4 20.1 reduce-scatter.8
  578.4 20.1 reduce-scatter.10
where the time goes:
time: 649 us; the launch traced here: 646 us
  blocking collectives  311 us (48%)
  local copies, waits for them, and re-layouts  87.6 us (13%)
  waiting for transfers between devices  83.8 us (13%)
  other arithmetic  72.8 us (11%)
  matrix products  39.1 us (6%)
  loops' own time  36.2 us (6%)
  between operations  15.2 us (2%)
    psum x3, blocking collectives, squares(): return lax.psum(jnp.sum(residual * residual, axis=(0, 2)), ('row', 'col'))  121 us
    reduce_scatter x4, waiting for transfers between devices, apply_operator(): lax.psum_scatter(gathered_sum, 'row', scatter_dimension=0, tiled=True)  83.7 us
    all_gather x4, blocking collectives, apply_operator(): pieces = lax.all_gather(vectors, 'col', axis=0, tiled=True)  83.5 us
    psum x2, blocking collectives, shards(): lax.psum(jnp.sum(direction * applied, axis=(0, 2)), ('row', 'col'))  78.6 us
    dot_general x48, matrix products, visit(): jnp.einsum('pab,psa->psb', weights, pieces[local_rows], precision=lax.Pre...  39.1 us
    another operation x4, loops' own time, apply_operator(): gathered_sum = lax.fori_loop(0, turns, visit, empty)  36.2 us
    convert_element_type x48, other arithmetic, group_weights(): inside = (indices < last).astype(jnp.float32)  30.5 us
    scatter-add x48, other arithmetic, visit(): return running.at[cols_group].add(product)  29.3 us
  transfers between devices with their start and end apart: 4, of which 4 were waited for; matrix products, arithmetic and copies ran while one was open for 0% of the time, Pallas kernels for 0%

commit v1 on v0

--- a/solution.py
+++ b/solution.py
@@ -54,7 +54,14 @@
 
     def apply_operator(vectors):
         empty = jnp.zeros((col_points.shape[0],) + vectors.shape[1:], jnp.float32)
-        pieces = lax.all_gather(vectors, "col", axis=0, tiled=True)
+        ring = [vectors]
+        for hop in range(15):
+            ring.append(lax.ppermute(ring[-1], "col", [(dev, (dev + 1) % 16) for dev in range(16)]))
+        pieces = jnp.roll(
+            jnp.concatenate(ring[::-1], axis=0),
+            (lax.axis_index("col") + 1) * ring[0].shape[0],
+            axis=0,
+        )
         number = pieces.shape[0]
         first, last, turns = pair_range(jnp.int32(0), number)
 

time: 649 us -> 909 us (1.40)
  waiting for transfers between devices: 83.8 us -> 429 us
  blocking collectives: 311 us -> 223 us
    ppermute x0 -> x60, waiting for transfers between devices: none -> 342 us  [apply_operator(): lax.ppermute(ring[-1], 'col', [(dev, (dev + 1) % 16) for dev in range(16)])]
    all_gather x4 -> x0, blocking collectives: 83.5 us -> none  [apply_operator(): pieces = lax.all_gather(vectors, 'col', axis=0, tiled=True)]
  transfers between devices with their start and end apart: 4 -> 64, of which waited for: 4 -> 63; matrix products, arithmetic and copies ran while one was open for 0% -> 1% of each run, Pallas kernels for 0% -> 0%
where the time goes in v1:
time: 909 us; the launch traced here: 907 us
  waiting for transfers between devices  429 us (47%)
  blocking collectives  223 us (25%)
  local copies, waits for them, and re-layouts  87.9 us (10%)
  other arithmetic  75.4 us (8%)
  matrix products  39.2 us (4%)
  loops' own time  36.2 us (4%)
  between operations  15.8 us (2%)
    ppermute x60, waiting for transfers between devices, apply_operator(): lax.ppermute(ring[-1], 'col', [(dev, (dev + 1) % 16) for dev in range(16)])  342 us
    psum x3, blocking collectives, squares(): return lax.psum(jnp.sum(residual * residual, axis=(0, 2)), ('row', 'col'))  121 us
    reduce_scatter x4, waiting for transfers between devices, apply_operator(): lax.psum_scatter(gathered_sum, 'row', scatter_dimension=0, tiled=True)  86.9 us
    psum x2, blocking collectives, shards(): lax.psum(jnp.sum(direction * applied, axis=(0, 2)), ('row', 'col'))  78.8 us
    dot_general x48, matrix products, visit(): jnp.einsum('pab,psa->psb', weights, pieces[local_rows], precision=lax.Pre...  39.2 us
    another operation x4, loops' own time, apply_operator(): gathered_sum = lax.fori_loop(0, turns, visit, empty)  36.2 us
    convert_element_type x48, other arithmetic, group_weights(): inside = (indices < last).astype(jnp.float32)  32.7 us
    scatter-add x48, other arithmetic, visit(): return running.at[cols_group].add(product)  29.3 us
  transfers between devices with their start and end apart: 64, of which 63 were waited for; matrix products, arithmetic and copies ran while one was open for 1% of the time, Pallas kernels for 0%

profile of v1, /device:TPU:0, one launch (start us, length us, event | category | flops | bytes accessed | tf_op | source)
XLA Modules:
  0.0 907.1 jit_solution(4417572746136524923)
XLA Ops:
  7.8 6.6 collective-permute-done
  14.4 5.9 collective-permute-done.1
  20.2 5.9 collective-permute-done.2
  26.1 5.9 collective-permute-done.3
  32.0 5.9 collective-permute-done.4
  37.8 5.9 collective-permute-done.5
  43.7 5.9 collective-permute-done.6
  49.5 5.9 collective-permute-done.7
  55.4 5.9 collective-permute-done.8
  61.3 5.9 collective-permute-done.9
  90.6 18.3 %all_gather.6 = f32[32,3,256]{2,1,0:T(4,128)S(1)} all-gather(f32[2,3,256]{2,1,0:T(4,128)S(1)} %copy.11), channel_id=1, replica_groups=mesh['row'=2,'col'=16] {'col'}, dimensions={0}, use_global_device_ids=true | all-gather | bytes 104448 | tf_op jit(solution)/shard_map/all_gather | solution.py:27
  116.4 56.3 %while.40 = (s32[]{:T(128)}, f32[4,8,256]{2,1,0:T(8,128)S(1)}, s32[]{:T(128)}, s32[]{:T(128)}, s32[65]{0:T(128)S(1)}, /*index=5*/s32[65]{0:T(128)S(1)}, f32[32,8...) while((s32[]{:T(128)}, f32[4,8,256]{2,1,0:T(8,128)S(1)}, ...), condition=%wide.region_5.7_spmd, body=%wide.region_3.6_spmd.sunk | while | flops 14687269 | bytes 213307 | solution.py:76
  173.4 22.5 %reduce-scatter.5.cloned.1.call-done = f32[2,8,256]{2,1,0:T(8,128)} async-done(((f32[4,8,256]{2,1,0:T(8,128)}), f32[2,8,256]{2,1,0:T(8,128)}) %reduce-scatter.5.cloned.1.call-update) | async-done | bytes 16400 | tf_op jit(solution)/shard_map/reduce_scatter | solution.py:77
  202.5 5.9 collective-permute-done.16
  208.3 5.9 collective-permute-done.17
  214.2 5.9 collective-permute-done.18
  220.0 5.9 collective-permute-done.19
  225.9 5.9 collective-permute-done.20
  231.8 5.9 collective-permute-done.21
  237.6 5.9 collective-permute-done.22
  243.5 5.9 collective-permute-done.23
  249.4 5.9 collective-permute-done.24
  255.2 5.9 collective-permute-done.25
  261.1 5.9 collective-permute-done.26
  266.9 5.9 collective-permute-done.27
  272.8 5.9 collective-permute-done.28
  278.7 5.9 collective-permute-done.29
  284.8 56.3 %while.41 = (s32[]{:T(128)}, f32[4,8,256]{2,1,0:T(8,128)S(1)}, s32[]{:T(128)}, s32[]{:T(128)}, s32[65]{0:T(128)S(1)}, /*index=5*/s32[65]{0:T(128)S(1)}, f32[32,8...) while((s32[]{:T(128)}, f32[4,8,256]{2,1,0:T(8,128)S(1)}, ...), condition=%wide.region_11.13_spmd, body=%wide.region_9.12_spmd.sunk | while | flops 14687269 | bytes 213307 | solution.py:76
  341.8 20.1 %reduce-scatter.7.cloned.1.call-done = f32[2,8,256]{2,1,0:T(8,128)} async-done(((f32[4,8,256]{2,1,0:T(8,128)}), f32[2,8,256]{2,1,0:T(8,128)}) %reduce-scatter.7.cloned.1.call-update) | async-done | bytes 16400 | tf_op jit(solution)/shard_map/reduce_scatter | solution.py:77
  362.8 39.3 %all-reduce.2 = (f32[8]{0:T(128)S(1)}, f32[8]{0:T(128)S(1)}) all-reduce(f32[8]{0:T(128)S(1)} %get-tuple-element.222, f32[8]{0:T(128)S(1)} %get-tuple-element.221), channel_id=1, replica_groups=mesh['row'=2,'col'=16] {'row','col'}, use_global_device_ids=true, to_apply=%region_8.10 | all-reduce | flops 16 | bytes 128 | tf_op jit(solution)/shard_map/psum | solution.py:23
  402.3 41.0 %psum.44 = f32[8]{0:T(128)S(1)} all-reduce(f32[8]{0:T(128)S(1)} %multiply_reduce_fusion.3), channel_id=1, replica_groups=mesh['row'=2,'col'=16] {'row','col'}, use_global_device_ids=true, to_apply=%region_16.18 | all-reduce | flops 8 | bytes 64 | tf_op jit(solution)/shard_map/psum | solution.py:23
  443.4 5.9 collective-permute-done.30
  449.2 5.9 collective-permute-done.31
  455.1 5.9 collective-permute-done.32
  460.9 5.9 collective-permute-done.33
  466.8 5.9 collective-permute-done.34
  472.7 5.9 collective-permute-done.35
  478.5 5.9 collective-permute-done.36
  484.4 5.9 collective-permute-done.37
  490.3 5.9 collective-permute-done.38
  496.1 5.9 collective-permute-done.39
  502.0 5.9 collective-permute-done.40
  507.8 5.9 collective-permute-done.41
  513.7 5.9 collective-permute-done.42
  519.6 5.9 collective-permute-done.43
  525.4 5.9 collective-permute-done.44
  531.6 56.3 %while.42 = (s32[]{:T(128)}, f32[4,8,256]{2,1,0:T(8,128)S(1)}, s32[]{:T(128)}, s32[]{:T(128)}, s32[65]{0:T(128)S(1)}, /*index=5*/s32[65]{0:T(128)S(1)}, f32[32,8...) while((s32[]{:T(128)}, f32[4,8,256]{2,1,0:T(8,128)S(1)}, ...), condition=%wide.region_19.21_spmd, body=%wide.region_17.20_spmd.sunk | while | flops 14687269 | bytes 213307 | solution.py:76
  588.5 22.2 %reduce-scatter.9.cloned.1.call-done = f32[2,8,256]{2,1,0:T(8,128)} async-done(((f32[4,8,256]{2,1,0:T(8,128)}), f32[2,8,256]{2,1,0:T(8,128)}) %reduce-scatter.9.cloned.1.call-update) | async-done | bytes 16400 | tf_op jit(solution)/shard_map/reduce_scatter | solution.py:77
  611.6 39.5 %psum.45 = f32[8]{0:T(128)S(1)} all-reduce(f32[8]{0:T(128)S(1)} %multiply_reduce_fusion.2), channel_id=1, replica_groups=mesh['row'=2,'col'=16] {'row','col'}, use_global_device_ids=true, to_apply=%region_22.24 | all-reduce | flops 8 | bytes 64 | tf_op jit(solution)/shard_map/psum | solution.py:86
  651.3 40.9 %psum.46 = f32[8]{0:T(128)S(1)} all-reduce(f32[8]{0:T(128)S(1)} %get-tuple-element.307), channel_id=1, replica_groups=mesh['row'=2,'col'=16] {'row','col'}, use_global_device_ids=true, to_apply=%region_24.26 | all-reduce | flops 8 | bytes 64 | tf_op jit(solution)/shard_map/psum | solution.py:23
  692.3 5.9 collective-permute-done.45
  698.2 5.9 collective-permute-done.46
  704.1 5.9 collective-permute-done.47
  709.9 5.9 collective-permute-done.48
  715.8 5.9 collective-permute-done.49
  745.1 5.9 collective-permute-done.54
  751.0 5.9 collective-permute-done.55
  756.8 5.9 collective-permute-done.56
  762.7 5.9 collective-permute-done.57
  768.5 5.9 collective-permute-done.58
  774.4 5.9 collective-permute-done.59
  780.5 56.3 %while.43 = (s32[]{:T(128)}, f32[4,8,256]{2,1,0:T(8,128)S(1)}, s32[]{:T(128)}, s32[]{:T(128)}, s32[65]{0:T(128)S(1)}, /*index=5*/s32[65]{0:T(128)S(1)}, f32[32,8...) while((s32[]{:T(128)}, f32[4,8,256]{2,1,0:T(8,128)S(1)}, ...), condition=%wide.region_27.29_spmd, body=%wide.region_25.28_spmd.sunk | while | flops 14687269 | bytes 213307 | solution.py:76
  837.5 22.2 %reduce-scatter.11.cloned.1.call-done = f32[2,8,256]{2,1,0:T(8,128)} async-done(((f32[4,8,256]{2,1,0:T(8,128)}), f32[2,8,256]{2,1,0:T(8,128)}) %reduce-scatter.11.cloned.1.call-update) | async-done | bytes 16400 | tf_op jit(solution)/shard_map/reduce_scatter | solution.py:77
  860.6 39.3 %psum.47 = f32[8]{0:T(128)S(1)} all-reduce(f32[8]{0:T(128)S(1)} %multiply_reduce_fusion), channel_id=1, replica_groups=mesh['row'=2,'col'=16] {'row','col'}, use_global_device_ids=true, to_apply=%region_30.32 | all-reduce | flops 8 | bytes 64 | tf_op jit(solution)/shard_map/psum | solution.py:86
  (1061 shorter events, 256.1 us)
Async XLA Ops:
  7.2 188.7 %reduce-scatter.5.cloned.1.call-start = ((), (), s32[]{:S(2)}) async-start(), calls=%async_computation.4 | async-start | bytes 49152 | tf_op jit(solution)/shard_map/reduce_scatter | solution.py:77
  7.2 7.2 collective-permute-start
  14.4 5.9 collective-permute-start.1
  20.2 5.9 collective-permute-start.2
  26.1 5.9 collective-permute-start.3
  32.0 5.9 collective-permute-start.4
  37.8 5.9 collective-permute-start.5
  43.7 5.9 collective-permute-start.6
  49.5 5.9 collective-permute-start.7
  55.4 5.9 collective-permute-start.8
  61.3 5.9 collective-permute-start.9
  67.1 5.9 collective-permute-start.10
  73.0 5.9 collective-permute-start.11
  78.8 5.9 collective-permute-start.12
  84.7 5.9 collective-permute-start.13
  90.6 24.9 %collective-permute-start.14 = (f32[2,8,256]{2,1,0:T(8,128)S(1)}, f32[2,8,256]{2,1,0:T(8,128)S(1)}, u32[]{:S(2)}, u32[]{:S(2)}) collective-permute-start(f32[2,8,256]{2,1,0:T(8,128)S(1)} %collective-permute-done.13), channel_id=1, source_target_pairs={{0,1},{1,2},{2,3},{3,4},{4,5},{5,6},{6,7},{7,8},{8,9},{9,10},{10,1... | collective-permute-start | bytes 49160 | tf_op jit(solution)/shard_map/ppermute | solution.py:59
  173.3 188.5 %reduce-scatter.7.cloned.1.call-start = ((), (), s32[]{:S(2)}) async-start(), calls=%async_computation.5 | async-start | bytes 49152 | tf_op jit(solution)/shard_map/reduce_scatter | solution.py:77
  196.6 5.9 collective-permute-start.15
  202.5 5.9 collective-permute-start.16
  208.3 5.9 collective-permute-start.17
  214.2 5.9 collective-permute-start.18
  220.0 5.9 collective-permute-start.19
  225.9 5.9 collective-permute-start.20
  231.8 5.9 collective-permute-start.21
  237.6 5.9 collective-permute-start.22
  243.5 5.9 collective-permute-start.23
  249.3 5.9 collective-permute-start.24
  255.2 5.9 collective-permute-start.25
  261.1 5.9 collective-permute-start.26
  266.9 5.9 collective-permute-start.27
  272.8 5.9 collective-permute-start.28
  278.7 5.9 collective-permute-start.29
  341.7 269.0 %reduce-scatter.9.cloned.1.call-start = ((), (), s32[]{:S(2)}) async-start(), calls=%async_computation.6 | async-start | bytes 49152 | tf_op jit(solution)/shard_map/reduce_scatter | solution.py:77
  443.4 5.9 collective-permute-start.30
  449.2 5.9 collective-permute-start.31
  455.1 5.9 collective-permute-start.32
  460.9 5.9 collective-permute-start.33
  466.8 5.9 collective-permute-start.34
  472.7 5.9 collective-permute-start.35
  478.5 5.9 collective-permute-start.36
  484.4 5.9 collective-permute-start.37
  490.3 5.9 collective-permute-start.38
  496.1 5.9 collective-permute-start.39
  502.0 5.9 collective-permute-start.40
  507.8 5.9 collective-permute-start.41
  513.7 5.9 collective-permute-start.42
  519.6 5.9 collective-permute-start.43
  525.4 5.9 collective-permute-start.44
  588.5 271.2 %reduce-scatter.11.cloned.1.call-start = ((), (), s32[]{:S(2)}) async-start(), calls=%async_computation.7 | async-start | bytes 49152 | tf_op jit(solution)/shard_map/reduce_scatter | solution.py:77
  692.3 5.9 collective-permute-start.45
  698.2 5.9 collective-permute-start.46
  704.1 5.9 collective-permute-start.47
  709.9 5.9 collective-permute-start.48
  715.8 5.9 collective-permute-start.49
  721.6 5.9 collective-permute-start.50
  727.5 5.9 collective-permute-start.51
  733.4 5.9 collective-permute-start.52
  739.2 5.9 collective-permute-start.53
  745.1 5.9 collective-permute-start.54
  751.0 5.9 collective-permute-start.55
  756.8 5.9 collective-permute-start.56
  762.7 5.9 collective-permute-start.57
  768.5 5.9 collective-permute-start.58
  774.4 5.9 collective-permute-start.59
  (11 other events, 177.0 us)
Sparse Core Ops, SparseCore 0:
  173.4 22.3 reduce-scatter.4
  341.8 19.9 reduce-scatter.6
  588.6 22.0 reduce-scatter.8
  837.6 22.0 reduce-scatter.10
